TPU v7x, 32 devices: a whole 2x2x4 slice. The times are simulated.
32 devices in a mesh: expert: 16 (over z, y, x), dp: 2 (over core).
Axes of the slice: x: 2, y: 2, z: 4, core: 2. Of those that a mesh axis runs over, the one named last changes fastest.
Arguments:
- events: bfloat16 [4096, 512], P(('expert', 'dp')), may hold values from -6 to 6
- gate_weights: float32 [4096, 2], P(('expert', 'dp')), may hold values from 0.1 to 1
- routes: int32 [4096, 2], P(('expert', 'dp')), may hold values from 0 to 15, all different within a row; in each aligned block of 128 rows (0 to 127, 128 to 255, ...) at most 32 rows name the same one
- session_of: int32 [4096], P(('expert', 'dp')), may hold values from 0 to 3, as said below
- partner: int32 [128], P(('expert', 'dp')), may hold values from 0 to 63, as said below
- expert_in: bfloat16 [16, 512, 1024], P('expert'), may hold values from -0.25 to 0.25
- expert_out: bfloat16 [16, 1024, 512], P('expert'), may hold values from -0.1875 to 0.1875
Outputs:
- mean_loss: float32 [], replicated
- grad_events: bfloat16 [4096, 512], P(('expert', 'dp'))
- grad_expert_in: bfloat16 [16, 512, 1024], P('expert', 'dp')
- grad_expert_out: bfloat16 [16, 1024, 512], P('expert', None, 'dp')
Inputs may be any that keep to these rules, and one draw needn't show every extreme that they name: `routes`: in every aligned block of 128 events (one device's events) no expert is named by more than 32 events, a bound that some block reaches; an event's two experts differ. `session_of`: within every aligned block of 128 events the numbers never fall, start at 0 and take every value up to 3. Within every in-batch set, partner pairs the sessions: partner[partner[i]] = i and partner[i] != i.
All inputs are finite; a program needn't handle non-finite values.
Results may differ from a plain program's by a relative error of at most 0.04.
Values may be sent and summed in bfloat16 or wider, within the bound.
A program may use at most 64 MiB of HBM per device.

v0:
```python
import math

import jax
import jax.numpy as jnp
from jax import lax
from jax.sharding import PartitionSpec as P

TAU = 0.07
NEG = -1e30
EPS = 1e-05


def silu_slope(preact):
    sigmoid = jax.nn.sigmoid(preact)
    return sigmoid * (1.0 + preact * (1.0 - sigmoid))


def left_product(left, right):
    return lax.dot_general(
        left, right, (((0,), (0,)), ((), ())), preferred_element_type=jnp.float32
    )


def body(events, gate_weights, routes, session_of, partner, expert_in, expert_out):
    experts = lax.axis_size("expert")
    copies = lax.axis_size("dp")
    ev_count, width = events.shape
    capacity = 4 * ev_count // experts
    targets = routes.reshape(-1)
    onehot = (targets[:, None] == jnp.arange(experts, dtype=jnp.int32)[None, :]).astype(jnp.int32)
    slot_index = jnp.sum((jnp.cumsum(onehot, axis=0) - onehot) * onehot, axis=1)
    source_event = jnp.arange(2 * ev_count, dtype=jnp.int32) // 2
    outbox = (
        jnp.zeros((experts, capacity, width), jnp.bfloat16)
        .at[targets, slot_index]
        .set(events[source_event])
    )
    inbox = lax.all_to_all(outbox, "expert", split_axis=0, concat_axis=0, tiled=True)
    inbox_rows = inbox.reshape(experts * capacity, width)
    preact = jnp.dot(inbox_rows, expert_in[0], preferred_element_type=jnp.float32)
    hidden = jax.nn.silu(preact).astype(jnp.bfloat16)
    output = jnp.dot(hidden, expert_out[0], preferred_element_type=jnp.float32).astype(jnp.bfloat16)
    returned = lax.all_to_all(
        output.reshape(experts, capacity, width), "expert", split_axis=0, concat_axis=0, tiled=True
    )
    picked = returned[targets, slot_index].reshape(ev_count, 2, width).astype(jnp.float32)
    mixed = events.astype(jnp.float32) + jnp.sum(gate_weights[:, :, None] * picked, axis=1)
    sessions = partner.shape[0]
    member = (session_of[None, :] == jnp.arange(sessions, dtype=jnp.int32)[:, None]).astype(
        jnp.float32
    )
    counts = jnp.sum(member, axis=1)
    pooled = jnp.dot(member, mixed, precision=lax.Precision.HIGHEST) / counts[:, None]
    emb_float = pooled.astype(jnp.bfloat16).astype(jnp.float32)
    rscale = lax.rsqrt(jnp.mean(emb_float * emb_float, axis=1) + EPS)
    unit = emb_float * rscale[:, None]
    zemb = unit.astype(jnp.bfloat16)
    everyone = lax.all_gather(zemb, "expert", axis=0, tiled=True)
    batch = everyone.shape[0]
    total_sessions = batch * copies
    scale = 1.0 / (math.sqrt(width) * TAU)
    logits = (
        lax.dot_general(
            zemb, everyone, (((1,), (1,)), ((), ())), preferred_element_type=jnp.float32
        )
        * scale
    )
    own_column = lax.axis_index("expert") * sessions + jnp.arange(sessions, dtype=jnp.int32)
    self_mask = jnp.arange(batch, dtype=jnp.int32)[None, :] == own_column[:, None]
    logits = jnp.where(self_mask, NEG, logits)
    highest = jnp.max(logits, axis=1)
    lse = highest + jnp.log(jnp.sum(jnp.exp(logits - highest[:, None]), axis=1))
    positive = jnp.take_along_axis(logits, partner[:, None], axis=1)[:, 0]
    mean_loss = lax.psum(jnp.sum(lse - positive), ("expert", "dp")) / total_sessions
    soft = jnp.exp(logits - lse[:, None]).astype(jnp.bfloat16)
    first = jnp.dot(soft, everyone, preferred_element_type=jnp.float32)
    second = lax.psum_scatter(left_product(soft, zemb), "expert", scatter_dimension=0, tiled=True)
    dunit = scale / total_sessions * (first + second - 2.0 * everyone[partner].astype(jnp.float32))
    dpooled = rscale[:, None] * (dunit - unit * jnp.mean(dunit * unit, axis=1, keepdims=True))
    dmixed = jnp.dot(member.T, dpooled / counts[:, None], precision=lax.Precision.HIGHEST)
    gated = (
        (gate_weights[:, :, None] * dmixed[:, None, :])
        .reshape(2 * ev_count, width)
        .astype(jnp.bfloat16)
    )
    grad_outbox = (
        jnp.zeros((experts, capacity, width), jnp.bfloat16).at[targets, slot_index].set(gated)
    )
    grad_inbox = lax.all_to_all(grad_outbox, "expert", split_axis=0, concat_axis=0, tiled=True)
    grad_rows = grad_inbox.reshape(experts * capacity, width)
    dhidden = lax.dot_general(
        grad_rows, expert_out[0], (((1,), (1,)), ((), ())), preferred_element_type=jnp.float32
    )
    dpre = (dhidden * silu_slope(preact)).astype(jnp.bfloat16)
    drows = lax.dot_general(
        dpre, expert_in[0], (((1,), (1,)), ((), ())), preferred_element_type=jnp.float32
    ).astype(jnp.bfloat16)
    grad_back = lax.all_to_all(
        drows.reshape(experts, capacity, width), "expert", split_axis=0, concat_axis=0, tiled=True
    )
    dpicked = grad_back[targets, slot_index].reshape(ev_count, 2, width).astype(jnp.float32)
    grad_events = (dmixed + jnp.sum(dpicked, axis=1)).astype(jnp.bfloat16)
    grad_in_rows = lax.psum_scatter(
        left_product(inbox_rows, dpre).astype(jnp.bfloat16), "dp", scatter_dimension=0, tiled=True
    )
    grad_out_rows = lax.psum_scatter(
        left_product(grad_rows, hidden).astype(jnp.bfloat16), "dp", scatter_dimension=0, tiled=True
    ).astype(jnp.float32)
    grad_expert_in = grad_in_rows[None]
    grad_expert_out = grad_out_rows.T.astype(jnp.bfloat16)[None]
    return (mean_loss, grad_events, grad_expert_in, grad_expert_out)


def solution(mesh):
    in_specs = (
        P(("expert", "dp"), None),
        P(("expert", "dp"), None),
        P(("expert", "dp"), None),
        P(("expert", "dp")),
        P(("expert", "dp")),
        P("expert", None, None),
        P("expert", None, None),
    )
    out_specs = (P(), P(("expert", "dp"), None), P("expert", "dp", None), P("expert", None, "dp"))
    return jax.shard_map(body, mesh=mesh, in_specs=in_specs, out_specs=out_specs, check_vma=False)
```

profile of v0, /device:TPU:0, one launch (start us, length us, event | category | flops | bytes accessed | tf_op | source)
XLA Modules:
  0.0 321.0 jit_solution(16424238332586870210)
XLA Ops:
  7.2 0.9 copy.28
  8.5 0.6 reduce-window.6
  9.4 2.1 gather_fusion
  11.6 13.7 %scatter_fusion = bf16[16,32,512]{2,1,0:T(8,128)(2,1)S(1)} fusion(bf16[16,32,512]{2,1,0:T(8,128)(2,1)S(1)} %broadcast.175.clone, s32[256]{0:T(256)S(1)} %bitcast.66, bf16[256,512]{1,0:T(8,128)(2,1)S(1)} %gather_fusion), kind=kCustom, calls=%fused_computation.5 | custom fusion | bytes 788480 | tf_op jit(solution)/shard_map/scatter | solution.py:36
  25.3 23.2 %all_to_all.20 = bf16[16,32,512]{2,1,0:T(8,128)(2,1)S(1)} all-to-all(bf16[16,32,512]{2,1,0:T(8,128)(2,1)S(1)} %scatter_fusion), channel_id=1, replica_groups=mesh['expert'=16,'dp'=2] {'expert'}, dimensions={0} | all-to-all | bytes 1048576 | tf_op jit(solution)/shard_map/all_to_all | solution.py:38
  48.5 2.3 multiply_convert_fusion.1
  50.8 1.5 convolution_convert_fusion.3
  52.3 3.9 %all-to-all-start.1 = ((bf16[16,32,512]{2,1,0:T(8,128)(2,1)}), bf16[16,32,512]{2,1,0:T(8,128)(2,1)S(1)}, u32[]{:S(2)}, u32[]{:S(2)}) async-start(bf16[16,32,512]{2,1,0:T(8,128)(2,1)} %bitcast.7), calls=%async_computation.1 | async-start | bytes 1048576 | tf_op jit(solution)/shard_map/all_to_all | solution.py:43
  56.6 14.0 %all-to-all-done.1 = bf16[16,32,512]{2,1,0:T(8,128)(2,1)S(1)} async-done(((bf16[16,32,512]{2,1,0:T(8,128)(2,1)}), bf16[16,32,512]{2,1,0:T(8,128)(2,1)S(1)}, u32[]{:S(2)}, u32[]{:S(2)}) %all-to-all-start.1) | async-done | bytes 524320 | tf_op jit(solution)/shard_map/all_to_all | solution.py:43
  70.7 2.1 gather_fusion.1
  73.1 0.7 multiply_reduce_fusion
  74.3 38.3 %all-gather = bf16[16,4,512]{2,1,0:T(4,128)(2,1)S(1)} all-gather(bf16[1,4,512]{2,1,0:T(4,128)(2,1)S(1)} %fusion.46), channel_id=1, replica_groups=mesh['expert'=16,'dp'=2] {'expert'}, dimensions={0}, use_global_device_ids=true | all-gather | bytes 69632 | tf_op jit(solution)/shard_map/all_gather | solution.py:58
  113.1 0.7 gather_fusion.4
  113.7 0.6 fusion.29
  114.3 0.9 fusion.30
  115.5 0.6 dynamic-slice
  116.8 0.6 gather_fusion.2
  117.3 99.4 %all-reduce.3.cloned.1.call-done = f32[64,512]{1,0:T(8,128)} async-done(((f32[64,512]{1,0:T(8,128)}), f32[64,512]{1,0:T(8,128)}) %all-reduce.3.cloned.1.call-update) | async-done | bytes 131088
  216.7 1.0 multiply_reduce_fusion.1
  218.8 13.7 %scatter_fusion.1 = bf16[16,32,512]{2,1,0:T(8,128)(2,1)S(1)} fusion(bf16[16,32,512]{2,1,0:T(8,128)(2,1)S(1)} %broadcast.175, s32[256]{0:T(256)S(1)} %bitcast.67, bf16[256,512]{1,0:T(8,128)(2,1)S(1)} %multiply_convert_fusion.2), kind=kCustom, calls=%fused_computation.6 | custom fusion | bytes 788480 | tf_op jit(solution)/shard_map/scatter | solution.py:87
  232.5 17.7 %all_to_all.21 = bf16[16,32,512]{2,1,0:T(8,128)(2,1)S(1)} all-to-all(bf16[16,32,512]{2,1,0:T(8,128)(2,1)S(1)} %scatter_fusion.1), channel_id=1, replica_groups=mesh['expert'=16,'dp'=2] {'expert'}, dimensions={0} | all-to-all | bytes 1048576 | tf_op jit(solution)/shard_map/all_to_all | solution.py:89
  250.2 3.0 convolution_convert_fusion
  253.5 2.7 multiply_convert_fusion
  256.1 1.0 copy-done.9
  257.2 1.7 convolution_convert_fusion.1
  258.9 2.8 convolution_convert_fusion.2
  261.7 4.1 %all-to-all-start.3 = ((bf16[16,32,512]{2,1,0:T(8,128)(2,1)}), bf16[16,32,512]{2,1,0:T(8,128)(2,1)S(1)}, u32[]{:S(2)}, u32[]{:S(2)}) async-start(bf16[16,32,512]{2,1,0:T(8,128)(2,1)} %bitcast.14), calls=%async_computation.3 | async-start | bytes 1048576 | tf_op jit(solution)/shard_map/all_to_all | solution.py:98
  265.8 41.1 %psum.7 = f32[]{:T(128)} all-reduce(f32[]{:T(128)} %get-tuple-element.20), channel_id=1, replica_groups=mesh['expert'=16,'dp'=2] {'expert','dp'}, use_global_device_ids=true, to_apply=%region_10.11 | all-reduce | flops 1 | bytes 8 | tf_op jit(solution)/shard_map/psum | solution.py:74
  307.5 2.1 gather_fusion.3
  310.0 0.6 reduce_sum.82
  310.6 0.7 add_convert_fusion
  311.3 2.0 copy.33
  (63 shorter events, 4.3 us)
Async XLA Ops:
  7.2 41.4 %copy-start = (bf16[1,512,1024]{2,1,0:T(8,128)(2,1)S(1)}, bf16[1,512,1024]{2,1,0:T(8,128)(2,1)}, u32[]{:S(2)}) copy-start(bf16[1,512,1024]{2,1,0:T(8,128)(2,1)} %param.12) | copy-start | bytes 3145732
  48.5 2.3 copy-start.5
  50.8 1.5 copy-start.8
  50.8 5.5 %copy-start.3 = (f32[128,2]{0,1:T(2,128)S(1)}, f32[128,2]{0,1:T(2,128)}, u32[]{:S(2)}) copy-start(f32[128,2]{0,1:T(2,128)} %param.8) | copy-start | bytes 3076
  50.8 5.7 %copy-start.4 = (s32[4]{0:T(128)S(1)}, s32[4]{0:T(128)}, u32[]{:S(2)}) copy-start(s32[4]{0:T(128)} %param.11) | copy-start | bytes 52
  50.8 5.7 %copy-start.2 = (s32[128]{0:T(128)S(1)}, s32[128]{0:T(128)}, u32[]{:S(2)}) copy-start(s32[128]{0:T(128)} %param.10) | copy-start | bytes 1540
  52.3 18.4 %all-to-all-start.1 = ((bf16[16,32,512]{2,1,0:T(8,128)(2,1)}), bf16[16,32,512]{2,1,0:T(8,128)(2,1)S(1)}, u32[]{:S(2)}, u32[]{:S(2)}) async-start(bf16[16,32,512]{2,1,0:T(8,128)(2,1)} %bitcast.7), calls=%async_computation.1 | async-start | bytes 1048576 | tf_op jit(solution)/shard_map/all_to_all | solution.py:43
  56.3 160.5 %all-reduce.3.cloned.1.call-start = ((), (), s32[]{:S(2)}) async-start(), calls=%async_computation.8 | async-start | bytes 262144
  56.3 17.5 %copy-start.1 = (bf16[128,512]{1,0:T(8,128)(2,1)S(1)}, bf16[128,512]{1,0:T(8,128)(2,1)}, u32[]{:S(2)}) copy-start(bf16[128,512]{1,0:T(8,128)(2,1)} %param.7) | copy-start | bytes 393220
  72.8 42.7 %copy-start.7 = (u32[32]{0:T(128)S(1)}, u32[32]{0:T(128)}, u32[]{:S(2)}) copy-start(u32[32]{0:T(128)} %constant.157) | copy-start | bytes 388
  115.3 196.0 %reduce-scatter.5.cloned.1.call-start = ((), (), s32[]{:S(2)}) async-start(), calls=%async_computation.7 | async-start | bytes 1572864 | tf_op jit(solution)/shard_map/reduce_scatter | solution.py:106
  250.2 3.3 %copy-start.6 = (bf16[1,1024,512]{2,1,0:T(8,128)(2,1)S(1)}, bf16[1,1024,512]{2,1,0:T(8,128)(2,1)}, u32[]{:S(2)}) copy-start(bf16[1,1024,512]{2,1,0:T(8,128)(2,1)} %param.13) | copy-start | bytes 3145732
  253.2 60.1 %reduce-scatter.3.cloned.1.call-start = ((), (), s32[]{:S(2)}) async-start(), calls=%async_computation.6 | async-start | bytes 1572864 | tf_op jit(solution)/shard_map/reduce_scatter | solution.py:103
  256.1 1.0 copy-start.9
  261.7 45.8 %all-to-all-start.3 = ((bf16[16,32,512]{2,1,0:T(8,128)(2,1)}), bf16[16,32,512]{2,1,0:T(8,128)(2,1)S(1)}, u32[]{:S(2)}, u32[]{:S(2)}) async-start(bf16[16,32,512]{2,1,0:T(8,128)(2,1)} %bitcast.14), calls=%async_computation.3 | async-start | bytes 1048576 | tf_op jit(solution)/shard_map/all_to_all | solution.py:98
Sparse Core Ops, SparseCore 0:
  115.4 101.2 all-reduce.2
  253.3 6.6 reduce-scatter.4
  262.9 9.5 reduce-scatter.2
where the time goes:
time: 322 us; the launch traced here: 321 us
  blocking collectives  120 us (37%)
  waiting for transfers between devices  113 us (35%)
  local copies, waits for them, and re-layouts  41.6 us (13%)
  matrix products  16.9 us (5%)
  between operations  16.5 us (5%)
  starting transfers between devices  8.31 us (3%)
  other arithmetic  3.88 us (1%)
    unnamed x4, waiting for transfers between devices  99.4 us
    psum x1, blocking collectives, body(): lax.psum(jnp.sum(lse - positive), ('expert', 'dp')) / total_sessions  41.1 us
    all_gather x1, blocking collectives, body(): everyone = lax.all_gather(zemb, 'expert', axis=0, tiled=True)  38.3 us
    all_to_all x1, blocking collectives, body(): lax.all_to_all(outbox, 'expert', split_axis=0, concat_axis=0, tiled=True)  23.2 us
    all_to_all x1, blocking collectives, body(): lax.all_to_all(grad_outbox, 'expert', split_axis=0, concat_axis=0, tiled=...  17.7 us
    all_to_all x1, waiting for transfers between devices, body(): lax.all_to_all(output.reshape(experts, capacity, width), 'expert', split_...  14 us
    scatter x1, local copies, waits for them, and re-layouts, body(): outbox = jnp.zeros((experts, capacity, width), jnp.bfloat16).at[targets,...  13.7 us
    scatter x1, local copies, waits for them, and re-layouts, body(): jnp.zeros((experts, capacity, width), jnp.bfloat16).at[targets, slot_index]  13.7 us
  transfers between devices with their start and end apart: 5, of which 2 were waited for; matrix products, arithmetic and copies ran while one was open for 5% of the time, Pallas kernels for 0%

commit v1 on v0

v1 whole, which is shorter than its diff:
```python
import functools
import math

import jax
import jax.numpy as jnp
from jax import lax
from jax.experimental import pallas as pl
from jax.experimental.pallas import tpu as pltpu
from jax.sharding import PartitionSpec as P

TAU = 0.07
NEG = -1e30
EPS = 1e-05
MESH = pl.DeviceIdType.MESH
F32 = jnp.float32
BF16 = jnp.bfloat16
SUB = 8
COUNT_LANE = 126
PARTNER_LANE = 127


def nn(left, right):
    return lax.dot_general(left, right, (((1,), (0,)), ((), ())), preferred_element_type=F32)


def nt(left, right):
    return lax.dot_general(left, right, (((1,), (1,)), ((), ())), preferred_element_type=F32)


def tn(left, right):
    return lax.dot_general(left, right, (((0,), (0,)), ((), ())), preferred_element_type=F32)


def halves(value):
    high = value.astype(BF16)
    return high, (value - high.astype(F32)).astype(BF16)


def iota(shape, dim):
    return lax.broadcasted_iota(jnp.int32, shape, dim)


def kernel(
    n, copies, cap, sessions,
    events, gates, routes, session_of, partner, w_in, w_out,
    loss_out, ge_out, gi_final, go_final,
    select, member_s, outbox, inbox, meta_out, meta_in, block, pre, hidden,
    pool_out, pool_in, emb_out, emb_in, emb_all, dm_all, dy_s, dpre_s, back_out, back_in,
    gi_out, gi_in, go_out, go_in, loss_buf,
    x_send, x_recv, m_send, m_recv, p_send, p_recv, e_send, e_recv, d_send, d_recv,
    gi_send, gi_recv, go_send, go_recv, l_send, l_recv,
):
    me = lax.axis_index("expert")
    dp = lax.axis_index("dp")
    ev, width = events.shape
    ff = w_in.shape[1]
    half_n = n // 2
    rows = half_n * cap
    ses_rows = half_n * SUB
    my_half = me // half_n
    far = 1 - my_half

    barrier = pltpu.get_barrier_semaphore()

    def greet(k, _):
        pl.semaphore_signal(
            barrier, inc=1, device_id={"expert": lax.rem(me + k, n)}, device_id_type=MESH
        )
        return 0

    lax.fori_loop(1, n, greet, 0)
    for k in range(1, copies):
        pl.semaphore_signal(
            barrier, inc=1, device_id={"dp": lax.rem(dp + k, copies)}, device_id_type=MESH
        )

    r0, r1 = routes[0:1, :], routes[1:2, :]
    g0, g1 = gates[0:1, :], gates[1:2, :]
    ids = iota((n, ev), 0)
    one0 = jnp.where(ids == r0, 1.0, 0.0).astype(F32)
    one1 = jnp.where(ids == r1, 1.0, 0.0).astype(F32)
    before = jnp.where(iota((ev, ev), 0) < iota((ev, ev), 1), 1.0, 0.0).astype(BF16)
    prefix = nn((one0 + one1).astype(BF16), before)
    p0 = r0 * cap + jnp.sum(prefix * one0, axis=0, keepdims=True).astype(jnp.int32)
    p1 = r1 * cap + jnp.sum(prefix * one1, axis=0, keepdims=True).astype(jnp.int32)
    place = iota((n * cap, ev), 0)
    at0, at1 = place == p0, place == p1
    select[...] = jnp.where(at0 | at1, 1.0, 0.0).astype(BF16)
    gate_at = jnp.where(at0, g0, jnp.where(at1, g1, 0.0))
    outbox[...] = nn(select[...], events[...]).astype(BF16)
    member = jnp.where(iota((SUB, ev), 0) == session_of[...], 1.0, 0.0).astype(F32)
    member_s[...] = member
    counts = jnp.sum(member, axis=1, keepdims=True)
    own_partner = jnp.sum(
        jnp.where(iota((SUB, sessions), 0) == iota((SUB, sessions), 1), partner[...], 0).astype(F32),
        axis=1, keepdims=True,
    )
    gate_high, gate_low = halves(gate_at)
    member_b = member.astype(BF16)
    lane = iota((SUB, 128), 1)
    wide = nt(member_b, gate_high) + nt(member_b, gate_low)
    for e in range(n):
        group, offset = divmod(e * cap, 128)
        tile = wide[:, group * 128 : (group + 1) * 128]
        if offset:
            tile = pltpu.roll(tile, 128 - offset, 1)
        tile = jnp.where(lane < cap, tile, 0.0)
        tile = jnp.where(lane == COUNT_LANE, counts, tile)
        meta_out[e] = jnp.where(lane == PARTNER_LANE, own_partner, tile)

    pl.semaphore_wait(barrier, n - 1 + copies - 1)

    def span(e):
        return pl.ds(pl.multiple_of(e * cap, cap), cap)

    def x_copy(target, source):
        return pltpu.make_async_remote_copy(
            src_ref=outbox.at[span(target)], dst_ref=inbox.at[span(source)],
            send_sem=x_send.at[target], recv_sem=x_recv.at[source],
            device_id={"expert": target}, device_id_type=MESH,
        )

    def m_copy(target, source):
        return pltpu.make_async_remote_copy(
            src_ref=meta_out.at[target], dst_ref=meta_in.at[source],
            send_sem=m_send.at[target], recv_sem=m_recv.at[source],
            device_id={"expert": target}, device_id_type=MESH,
        )

    def p_copy(target, source):
        return pltpu.make_async_remote_copy(
            src_ref=pool_out.at[target], dst_ref=pool_in.at[source],
            send_sem=p_send.at[target], recv_sem=p_recv.at[source],
            device_id={"expert": target}, device_id_type=MESH,
        )

    def e_copy(target, source):
        return pltpu.make_async_remote_copy(
            src_ref=emb_out, dst_ref=emb_in.at[source],
            send_sem=e_send.at[target], recv_sem=e_recv.at[source],
            device_id={"expert": target}, device_id_type=MESH,
        )

    def d_copy(target, source):
        return pltpu.make_async_remote_copy(
            src_ref=back_out.at[span(target)], dst_ref=back_in.at[span(source)],
            send_sem=d_send.at[target], recv_sem=d_recv.at[source],
            device_id={"expert": target}, device_id_type=MESH,
        )

    def in_far(i):
        return far * half_n + lax.rem(me + i, half_n)

    def in_near(i):
        return my_half * half_n + lax.rem(me + i, half_n)

    def each_far(act):
        def step(i, _):
            act(in_far(i))
            return 0

        lax.fori_loop(0, half_n, step, 0)

    def each_near(act):
        def step(i, _):
            act(in_near(i))
            return 0

        lax.fori_loop(1, half_n, step, 0)

    def send_x(t):
        m_copy(t, me).start()
        x_copy(t, me).start()

    each_far(send_x)
    each_near(send_x)
    inbox[span(me), :] = outbox[span(me), :]
    meta_in[me] = meta_out[me]

    event_sum = nn(member_b, events[...])

    def wait_x(s):
        m_copy(s, s).wait_recv()
        x_copy(s, s).wait_recv()

    def forward(half):
        at = pl.ds(pl.multiple_of(half * rows, rows), rows)
        preact = nn(inbox[at, :], w_in[...])
        pre[at, :] = preact
        act = (preact / (1.0 + jnp.exp(-preact))).astype(BF16)
        hidden[at, :] = act
        y = nn(act, w_out[...]).astype(BF16)
        table = meta_in[pl.ds(half * half_n, half_n)].reshape(ses_rows, 128)
        spread = jnp.where(iota((128, rows), 0) == iota((128, rows), 1) % cap, 1.0, 0.0).astype(BF16)
        high, low = halves(table)
        full = nn(high, spread) + nn(low, spread)
        full = jnp.where(iota((ses_rows, rows), 0) // SUB == iota((ses_rows, rows), 1) // cap, full, 0.0)
        block[half] = full
        high, low = halves(full)
        part = nn(high, y) + nn(low, y)
        for j in range(half_n):
            pool_out[half * half_n + j] = part[SUB * j : SUB * j + sessions]

    each_near(wait_x)
    forward(my_half)
    each_near(lambda t: p_copy(t, me).start())
    pool_in[me] = pool_out[me]
    each_far(wait_x)
    forward(far)
    each_far(lambda t: p_copy(t, me).start())

    each_near(lambda s: p_copy(s, s).wait_recv())
    each_far(lambda s: p_copy(s, s).wait_recv())
    total = event_sum[0:sessions] + jnp.sum(pool_in[...], axis=0)
    emb = (total / counts[0:sessions]).astype(BF16).astype(F32)
    emb_out[...] = emb
    each_far(lambda t: e_copy(t, me).start())
    each_near(lambda t: e_copy(t, me).start())
    emb_in[me] = emb
    each_near(lambda s: e_copy(s, s).wait_recv())
    each_far(lambda s: e_copy(s, s).wait_recv())

    blank = jnp.zeros((SUB - sessions, width), F32)
    for e in range(n):
        emb_all[SUB * e : SUB * (e + 1), :] = jnp.concatenate([emb_in[e], blank], axis=0)
    batch = n * SUB
    emb = emb_all[...]
    scale = 1.0 / (math.sqrt(width) * TAU)
    all_sessions = n * sessions * copies
    rscale = lax.rsqrt(jnp.mean(emb * emb, axis=1, keepdims=True) + EPS)
    unit = emb * rscale
    zemb = unit.astype(BF16)
    table = meta_in[...].reshape(batch, 128)
    table_lane = iota((batch, 128), 1)
    row1 = iota((batch, 1), 0)
    real1 = row1 % SUB < sessions
    number = jnp.sum(jnp.where(table_lane == COUNT_LANE, table, 0.0), axis=1, keepdims=True)
    number = jnp.where(real1, number, 1.0)
    mate = jnp.sum(jnp.where(table_lane == PARTNER_LANE, table, 0.0), axis=1, keepdims=True)
    mate = mate.astype(jnp.int32)
    mate = mate // sessions * SUB + mate % sessions
    row = iota((batch, batch), 0)
    column = iota((batch, batch), 1)
    row_real = row % SUB < sessions
    logits = nt(zemb, zemb) * scale
    logits = jnp.where((row == column) | (column % SUB >= sessions), NEG, logits)
    highest = jnp.max(logits, axis=1, keepdims=True)
    lse = highest + jnp.log(jnp.sum(jnp.exp(logits - highest), axis=1, keepdims=True))
    is_mate = (column == mate) & row_real
    positive = jnp.sum(jnp.where(is_mate, logits, 0.0), axis=1, keepdims=True)
    loss = jnp.sum(jnp.where(real1, lse - positive, 0.0), axis=0, keepdims=True)
    loss_buf[dp] = jnp.broadcast_to(loss, (SUB, 128))
    soft = jnp.where(row_real, jnp.exp(logits - lse), 0.0).astype(BF16)
    mates = jnp.where(is_mate, 1.0, 0.0).astype(BF16)
    dunit = nn(soft, zemb) + tn(soft, zemb) - 2.0 * nn(mates, zemb)
    dunit = (scale / all_sessions) * dunit
    dpooled = rscale * (dunit - unit * jnp.mean(dunit * unit, axis=1, keepdims=True))
    dm_all[...] = dpooled / number

    def backward(half):
        at = pl.ds(pl.multiple_of(half * rows, rows), rows)
        high, low = halves(dm_all[pl.ds(pl.multiple_of(half * ses_rows, ses_rows), ses_rows), :])
        full = block[half]
        hot = jnp.where(full != 0.0, 1.0, 0.0).astype(BF16)
        dmix = tn(hot, high) + tn(hot, low)
        high, low = halves(full)
        ones = jnp.ones((ses_rows, width), BF16)
        dy = (dmix * (tn(high, ones) + tn(low, ones))).astype(BF16)
        dy_s[at, :] = dy
        preact = pre[at, :]
        sig = 1.0 / (1.0 + jnp.exp(-preact))
        dpre = (nt(dy, w_out[...]) * (sig * (1.0 + preact * (1.0 - sig)))).astype(BF16)
        dpre_s[at, :] = dpre
        back_out[at, :] = nt(dpre, w_in[...]).astype(BF16)

    backward(far)
    each_far(lambda t: d_copy(t, me).start())
    backward(my_half)
    each_near(lambda t: d_copy(t, me).start())
    back_in[span(me), :] = back_out[span(me), :]

    def dp_copies(peer, source):
        device = {"dp": peer}
        return (
            pltpu.make_async_remote_copy(
                src_ref=gi_out.at[peer], dst_ref=gi_in.at[source],
                send_sem=gi_send.at[peer], recv_sem=gi_recv.at[source],
                device_id=device, device_id_type=MESH,
            ),
            pltpu.make_async_remote_copy(
                src_ref=go_out.at[peer], dst_ref=go_in.at[source],
                send_sem=go_send.at[peer], recv_sem=go_recv.at[source],
                device_id=device, device_id_type=MESH,
            ),
            pltpu.make_async_remote_copy(
                src_ref=loss_buf.at[dp], dst_ref=loss_buf.at[source],
                send_sem=l_send.at[peer], recv_sem=l_recv.at[source],
                device_id=device, device_id_type=MESH,
            ),
        )

    peers = [lax.rem(dp + k, copies) for k in range(1, copies)]
    for peer in peers:
        dp_copies(peer, dp)[2].start()
    part = width // copies
    for c in range(copies):
        gi_out[c] = tn(inbox[:, c * part : (c + 1) * part], dpre_s[...]).astype(BF16)
    for peer in peers:
        dp_copies(peer, dp)[0].start()
    for c in range(copies):
        go_out[c] = tn(hidden[...], dy_s[:, c * part : (c + 1) * part]).astype(BF16)
    for peer in peers:
        dp_copies(peer, dp)[1].start()

    own = dm_all[pl.ds(pl.multiple_of(me * SUB, SUB), SUB), :]
    high, low = halves(own)
    member_b = member_s[...].astype(BF16)
    dmixed = tn(member_b, high) + tn(member_b, low)
    acc = gi_out[dp].astype(F32)
    for peer in peers:
        dp_copies(peer, peer)[0].wait_recv()
        acc = acc + gi_in[peer].astype(F32)
    gi_final[...] = acc.astype(BF16)
    acc = go_out[dp].astype(F32)
    for peer in peers:
        dp_copies(peer, peer)[1].wait_recv()
        acc = acc + go_in[peer].astype(F32)
    go_final[...] = acc.astype(BF16)
    for peer in peers:
        dp_copies(peer, peer)[2].wait_recv()
    loss_out[...] = (jnp.sum(loss_buf[...], axis=0) / all_sessions)[0:1, 0:1]

    each_near(lambda s: d_copy(s, s).wait_recv())
    each_far(lambda s: d_copy(s, s).wait_recv())
    ge_out[...] = (dmixed + tn(select[...], back_in[...])).astype(BF16)

    def drain(t):
        m_copy(t, me).wait_send()
        x_copy(t, me).wait_send()
        p_copy(t, me).wait_send()
        e_copy(t, me).wait_send()
        d_copy(t, me).wait_send()

    each_far(drain)
    each_near(drain)
    for peer in peers:
        for copy in dp_copies(peer, dp):
            copy.wait_send()


def body(n, copies, events, gate_weights, routes, session_of, partner, expert_in, expert_out):
    ev, width = events.shape
    ff = expert_in.shape[2]
    cap = 4 * ev // n
    sessions = partner.shape[0]
    part = width // copies
    slots = n * cap
    dma = pltpu.SemaphoreType.DMA
    vmem = pl.BlockSpec(memory_space=pltpu.VMEM)
    loss, ge, gi, go = pl.pallas_call(
        functools.partial(kernel, n, copies, cap, sessions),
        out_shape=(
            jax.ShapeDtypeStruct((1, 1), F32),
            jax.ShapeDtypeStruct((ev, width), BF16),
            jax.ShapeDtypeStruct((part, ff), BF16),
            jax.ShapeDtypeStruct((ff, part), BF16),
        ),
        in_specs=[vmem] * 7,
        out_specs=(vmem,) * 4,
        scratch_shapes=[
            pltpu.VMEM((slots, ev), BF16),
            pltpu.VMEM((SUB, ev), F32),
            pltpu.VMEM((slots, width), BF16),
            pltpu.VMEM((slots, width), BF16),
            pltpu.VMEM((n, SUB, 128), F32),
            pltpu.VMEM((n, SUB, 128), F32),
            pltpu.VMEM((2, n // 2 * SUB, slots // 2), F32),
            pltpu.VMEM((slots, ff), F32),
            pltpu.VMEM((slots, ff), BF16),
            pltpu.VMEM((n, sessions, width), F32),
            pltpu.VMEM((n, sessions, width), F32),
            pltpu.VMEM((sessions, width), F32),
            pltpu.VMEM((n, sessions, width), F32),
            pltpu.VMEM((n * SUB, width), F32),
            pltpu.VMEM((n * SUB, width), F32),
            pltpu.VMEM((slots, width), BF16),
            pltpu.VMEM((slots, ff), BF16),
            pltpu.VMEM((slots, width), BF16),
            pltpu.VMEM((slots, width), BF16),
            pltpu.VMEM((copies, part, ff), BF16),
            pltpu.VMEM((copies, part, ff), BF16),
            pltpu.VMEM((copies, ff, part), BF16),
            pltpu.VMEM((copies, ff, part), BF16),
            pltpu.VMEM((copies, SUB, 128), F32),
        ]
        + [dma((n,))] * 10
        + [dma((copies,))] * 6,
        compiler_params=pltpu.CompilerParams(collective_id=0, has_side_effects=True, vmem_limit_bytes=50 << 20),
        name="session_moe",
    )(
        events, gate_weights.T, routes.T, session_of.reshape(1, ev), partner.reshape(1, sessions),
        expert_in[0], expert_out[0],
    )
    return loss.reshape(()), ge, gi[None], go[None]


def solution(mesh):
    in_specs = (
        P(("expert", "dp"), None),
        P(("expert", "dp"), None),
        P(("expert", "dp"), None),
        P(("expert", "dp")),
        P(("expert", "dp")),
        P("expert", None, None),
        P("expert", None, None),
    )
    out_specs = (P(), P(("expert", "dp"), None), P("expert", "dp", None), P("expert", None, "dp"))
    step = functools.partial(body, mesh.shape["expert"], mesh.shape["dp"])
    return jax.shard_map(step, mesh=mesh, in_specs=in_specs, out_specs=out_specs, check_vma=False)
```

time: 322 us -> 57.3 us (0.18)
  blocking collectives: 120 us -> 0 us
  waiting for transfers between devices: 113 us -> 0 us
  Pallas kernels: 0 us -> 48.4 us
  local copies, waits for them, and re-layouts: 41.6 us -> 6.28 us
  matrix products: 16.9 us -> 0 us
  between operations: 16.5 us -> 2.37 us
  starting transfers between devices: 8.31 us -> 0 us
  other arithmetic: 3.88 us -> 0 us
    unnamed x4 -> x0, waiting for transfers between devices: 99.4 us -> none
    pallas_call x0 -> x1, Pallas kernels: none -> 48.4 us  [body(): pl.pallas_call(functools.partial(kernel, n, copies, cap, sessions), out_s...]
    psum x1 -> x0, blocking collectives: 41.1 us -> none  [body(): lax.psum(jnp.sum(lse - positive), ('expert', 'dp')) / total_sessions]
    all_to_all x2 -> x0, blocking collectives: 40.9 us -> none  [the longest x1 23.2 us: body(): lax.all_to_all(outbox, 'expert', split_axis=0, concat_axis=0, tiled=True)]
    all_gather x1 -> x0, blocking collectives: 38.3 us -> none  [body(): everyone = lax.all_gather(zemb, 'expert', axis=0, tiled=True)]
    scatter x2 -> x0, local copies, waits for them, and re-layouts: 27.3 us -> none  [the longest x1 13.7 us: body(): outbox = jnp.zeros((experts, capacity, width), jnp.bfloat16).at[targets,...]
    dot_general x11 -> x0, matrix products: 16.9 us -> none  [the longest x3 5.68 us: left_product(): lax.dot_general(left, right, (((0,), (0,)), ((), ())), preferred_element_...]
    all_to_all x2 -> x0, waiting for transfers between devices: 14 us -> none  [the longest x1 14 us: body(): lax.all_to_all(output.reshape(experts, capacity, width), 'expert', split_...]
  transfers between devices with their start and end apart: 5 -> 0, of which waited for: 2 -> 0; matrix products, arithmetic and copies ran while one was open for 5% -> 0% of each run, Pallas kernels for 0% -> 0%
where the time goes in v1:
time: 57.3 us; the launch traced here: 57 us
  Pallas kernels  48.4 us (84%)
  local copies, waits for them, and re-layouts  6.28 us (11%)
  between operations  2.37 us (4%)
    pallas_call x1, Pallas kernels, body(): pl.pallas_call(functools.partial(kernel, n, copies, cap, sessions), out_s...  48.4 us
    unnamed x17, local copies, waits for them, and re-layouts  6.28 us

profile of v1, /device:TPU:0, one launch (start us, length us, event | category | flops | bytes accessed | tf_op | source)
XLA Modules:
  0.0 57.0 jit_solution(5083190122049088319)
XLA Ops:
  0.6 0.0 copy-start.4
  0.6 0.0 copy-start.6
  0.7 0.0 copy-start.3
  0.7 0.0 copy-start.5
  0.7 0.6 %copy-done.4 = s32[128,2]{0,1:T(2,128)S(1)} copy-done((s32[128,2]{0,1:T(2,128)S(1)}, s32[128,2]{0,1:T(2,128)}, u32[]{:S(2)}) %copy-start.4) | copy-done | bytes 1048
  1.3 0.0 copy-done.6
  1.3 0.0 copy-done.3
  1.3 0.0 copy-done.5
  1.3 0.0 copy-start
  1.3 1.2 %copy-done = bf16[1,512,1024]{2,1,0:T(8,128)(2,1)S(1)} copy-done((bf16[1,512,1024]{2,1,0:T(8,128)(2,1)S(1)}, bf16[1,512,1024]{2,1,0:T(8,128)(2,1)}, u32[]{:S(2)}) %copy-start) | copy-done | bytes 1048600
  2.6 0.0 copy-start.1
  2.6 1.2 %copy-done.1 = bf16[1,1024,512]{2,1,0:T(8,128)(2,1)S(1)} copy-done((bf16[1,1024,512]{2,1,0:T(8,128)(2,1)S(1)}, bf16[1,1024,512]{2,1,0:T(8,128)(2,1)}, u32[]{:S(2)}) %copy-start.1) | copy-done | bytes 1048600
  3.8 0.0 copy-start.2
  3.8 0.9 %copy-done.2 = bf16[128,512]{1,0:T(8,128)(2,1)S(1)} copy-done((bf16[128,512]{1,0:T(8,128)(2,1)S(1)}, bf16[128,512]{1,0:T(8,128)(2,1)}, u32[]{:S(2)}) %copy-start.2) | copy-done | bytes 131096
  4.7 48.4 %session_moe.1 = (f32[1,1]{1,0:T(1,128)}, bf16[128,512]{1,0:T(8,128)(2,1)S(1)}, bf16[256,1024]{1,0:T(8,128)(2,1)S(1)}, bf16[1024,256]{1,0:T(8,128)(2,1)S(1)}) custom-call(bf16[128,512]{1,0:T(8,128)(2,1)S(1)} %copy-done.2, f32[2,128]{1,0:T(2,128)S(1)} %bitcast.13, s32[2,128]{1,0:T(2,128)S(1)} %bitcast.14, s32[1,128]{1,0:T(1,128)S(1)} %bitcast.15, ...), custom_call_target="tpu_custom_call" | custom-call | tf_op jit(solution)/shard_map/session_moe/pallas_call | solution.py:360
  53.7 0.7 %copy.16 = bf16[128,512]{1,0:T(8,128)(2,1)} copy(bf16[128,512]{1,0:T(8,128)(2,1)S(1)} %get-tuple-element.17) | data formatting | bytes 262144
  54.3 0.8 %copy.17 = bf16[1,256,1024]{2,1,0:T(8,128)(2,1)} copy(bf16[1,256,1024]{2,1,0:T(8,128)(2,1)S(1)} %bitcast.12) | data formatting | bytes 1048576
  55.1 0.8 %copy.18 = bf16[1,1024,256]{2,1,0:T(8,128)(2,1)} copy(bf16[1,1024,256]{2,1,0:T(8,128)(2,1)S(1)} %bitcast.11) | data formatting | bytes 1048576
Async XLA Ops:
  0.6 0.7 %copy-start.4 = (s32[128,2]{0,1:T(2,128)S(1)}, s32[128,2]{0,1:T(2,128)}, u32[]{:S(2)}) copy-start(s32[128,2]{0,1:T(2,128)} %param.9) | copy-start | bytes 3076
  0.6 0.7 %copy-start.6 = (s32[4]{0:T(128)S(1)}, s32[4]{0:T(128)}, u32[]{:S(2)}) copy-start(s32[4]{0:T(128)} %param.11) | copy-start | bytes 52
  0.7 0.7 %copy-start.3 = (f32[128,2]{0,1:T(2,128)S(1)}, f32[128,2]{0,1:T(2,128)}, u32[]{:S(2)}) copy-start(f32[128,2]{0,1:T(2,128)} %param.8) | copy-start | bytes 3076
  0.7 0.7 %copy-start.5 = (s32[128]{0:T(128)S(1)}, s32[128]{0:T(128)}, u32[]{:S(2)}) copy-start(s32[128]{0:T(128)} %param.10) | copy-start | bytes 1540
  1.3 1.2 %copy-start = (bf16[1,512,1024]{2,1,0:T(8,128)(2,1)S(1)}, bf16[1,512,1024]{2,1,0:T(8,128)(2,1)}, u32[]{:S(2)}) copy-start(bf16[1,512,1024]{2,1,0:T(8,128)(2,1)} %param.12) | copy-start | bytes 3145732
  2.6 1.2 %copy-start.1 = (bf16[1,1024,512]{2,1,0:T(8,128)(2,1)S(1)}, bf16[1,1024,512]{2,1,0:T(8,128)(2,1)}, u32[]{:S(2)}) copy-start(bf16[1,1024,512]{2,1,0:T(8,128)(2,1)} %param.13) | copy-start | bytes 3145732
  3.8 0.9 %copy-start.2 = (bf16[128,512]{1,0:T(8,128)(2,1)S(1)}, bf16[128,512]{1,0:T(8,128)(2,1)}, u32[]{:S(2)}) copy-start(bf16[128,512]{1,0:T(8,128)(2,1)} %events.1) | copy-start | bytes 393220

commit v2 on v1

--- a/solution.py
+++ b/solution.py
@@ -15,6 +15,7 @@
 F32 = jnp.float32
 BF16 = jnp.bfloat16
 SUB = 8
+VMEM_ALL = 67043328
 COUNT_LANE = 126
 PARTNER_LANE = 127
 
@@ -42,11 +43,12 @@
 
 def kernel(
     n, copies, cap, sessions,
-    events, gates, routes, session_of, partner, w_in, w_out,
-    loss_out, ge_out, gi_final, go_final,
+    events_h, gates_h, routes_h, session_h, partner_h, w_in_h, w_out_h,
+    loss_out, ge_h, gi_h, go_h,
     select, member_s, outbox, inbox, meta_out, meta_in, block, pre, hidden,
     pool_out, pool_in, emb_out, emb_in, emb_all, dm_all, dy_s, dpre_s, back_out, back_in,
-    gi_out, gi_in, go_out, go_in, loss_buf,
+    gi_out, gi_in, go_out, go_in, loss_buf, gate_cols,
+    events, gates, routes, session_of, partner, w_in, w_out, ge_out, gi_final, go_final, fetch, store,
     x_send, x_recv, m_send, m_recv, p_send, p_recv, e_send, e_recv, d_send, d_recv,
     gi_send, gi_recv, go_send, go_recv, l_send, l_recv,
 ):
@@ -60,6 +62,17 @@
     my_half = me // half_n
     far = 1 - my_half
 
+    fetches = [
+        pltpu.make_async_copy(source, target, fetch.at[i])
+        for i, (source, target) in enumerate(
+            (
+                (routes_h, routes), (gates_h, gates), (session_h, session_of), (partner_h, partner),
+                (events_h, events), (w_in_h, w_in), (w_out_h, w_out),
+            )
+        )
+    ]
+    for copy in fetches[:5]:
+        copy.start()
     barrier = pltpu.get_barrier_semaphore()
 
     def greet(k, _):
@@ -73,6 +86,11 @@
         pl.semaphore_signal(
             barrier, inc=1, device_id={"dp": lax.rem(dp + k, copies)}, device_id_type=MESH
         )
+
+    for copy in fetches[5:]:
+        copy.start()
+    for copy in fetches[:4]:
+        copy.wait()
 
     r0, r1 = routes[0:1, :], routes[1:2, :]
     g0, g1 = gates[0:1, :], gates[1:2, :]
@@ -87,6 +105,7 @@
     at0, at1 = place == p0, place == p1
     select[...] = jnp.where(at0 | at1, 1.0, 0.0).astype(BF16)
     gate_at = jnp.where(at0, g0, jnp.where(at1, g1, 0.0))
+    fetches[4].wait()
     outbox[...] = nn(select[...], events[...]).astype(BF16)
     member = jnp.where(iota((SUB, ev), 0) == session_of[...], 1.0, 0.0).astype(F32)
     member_s[...] = member
@@ -199,20 +218,33 @@
         high, low = halves(full)
         part = nn(high, y) + nn(low, y)
         for j in range(half_n):
-            pool_out[half * half_n + j] = part[SUB * j : SUB * j + sessions]
-
+            pool_out[half * half_n + j] = part[SUB * j : SUB * j + sessions].astype(BF16)
+
+    def prepare(half):
+        at = pl.ds(pl.multiple_of(half * rows, rows), rows)
+        preact = pre[at, :]
+        sig = 1.0 / (1.0 + jnp.exp(-preact))
+        pre[at, :] = sig * (1.0 + preact * (1.0 - sig))
+        high, low = halves(block[half])
+        ones = jnp.ones((ses_rows, width), BF16)
+        gate_cols[at, :] = tn(high, ones) + tn(low, ones)
+
+    fetches[5].wait()
+    fetches[6].wait()
     each_near(wait_x)
     forward(my_half)
     each_near(lambda t: p_copy(t, me).start())
     pool_in[me] = pool_out[me]
+    prepare(my_half)
     each_far(wait_x)
     forward(far)
     each_far(lambda t: p_copy(t, me).start())
+    prepare(far)
 
     each_near(lambda s: p_copy(s, s).wait_recv())
     each_far(lambda s: p_copy(s, s).wait_recv())
-    total = event_sum[0:sessions] + jnp.sum(pool_in[...], axis=0)
-    emb = (total / counts[0:sessions]).astype(BF16).astype(F32)
+    total = event_sum[0:sessions] + jnp.sum(pool_in[...].astype(F32), axis=0)
+    emb = (total / counts[0:sessions]).astype(BF16)
     emb_out[...] = emb
     each_far(lambda t: e_copy(t, me).start())
     each_near(lambda t: e_copy(t, me).start())
@@ -222,7 +254,7 @@
 
     blank = jnp.zeros((SUB - sessions, width), F32)
     for e in range(n):
-        emb_all[SUB * e : SUB * (e + 1), :] = jnp.concatenate([emb_in[e], blank], axis=0)
+        emb_all[SUB * e : SUB * (e + 1), :] = jnp.concatenate([emb_in[e].astype(F32), blank], axis=0)
     batch = n * SUB
     emb = emb_all[...]
     scale = 1.0 / (math.sqrt(width) * TAU)
@@ -260,16 +292,10 @@
     def backward(half):
         at = pl.ds(pl.multiple_of(half * rows, rows), rows)
         high, low = halves(dm_all[pl.ds(pl.multiple_of(half * ses_rows, ses_rows), ses_rows), :])
-        full = block[half]
-        hot = jnp.where(full != 0.0, 1.0, 0.0).astype(BF16)
-        dmix = tn(hot, high) + tn(hot, low)
-        high, low = halves(full)
-        ones = jnp.ones((ses_rows, width), BF16)
-        dy = (dmix * (tn(high, ones) + tn(low, ones))).astype(BF16)
+        hot = jnp.where(block[half] != 0.0, 1.0, 0.0).astype(BF16)
+        dy = ((tn(hot, high) + tn(hot, low)) * gate_cols[at, :]).astype(BF16)
         dy_s[at, :] = dy
-        preact = pre[at, :]
-        sig = 1.0 / (1.0 + jnp.exp(-preact))
-        dpre = (nt(dy, w_out[...]) * (sig * (1.0 + preact * (1.0 - sig)))).astype(BF16)
+        dpre = (nt(dy, w_out[...]) * pre[at, :]).astype(BF16)
         dpre_s[at, :] = dpre
         back_out[at, :] = nt(dpre, w_in[...]).astype(BF16)
 
@@ -321,11 +347,17 @@
         dp_copies(peer, peer)[0].wait_recv()
         acc = acc + gi_in[peer].astype(F32)
     gi_final[...] = acc.astype(BF16)
+    stores = [
+        pltpu.make_async_copy(source, target, store.at[i])
+        for i, (source, target) in enumerate(((gi_final, gi_h), (go_final, go_h), (ge_out, ge_h)))
+    ]
+    stores[0].start()
     acc = go_out[dp].astype(F32)
     for peer in peers:
         dp_copies(peer, peer)[1].wait_recv()
         acc = acc + go_in[peer].astype(F32)
     go_final[...] = acc.astype(BF16)
+    stores[1].start()
     for peer in peers:
         dp_copies(peer, peer)[2].wait_recv()
     loss_out[...] = (jnp.sum(loss_buf[...], axis=0) / all_sessions)[0:1, 0:1]
@@ -333,6 +365,7 @@
     each_near(lambda s: d_copy(s, s).wait_recv())
     each_far(lambda s: d_copy(s, s).wait_recv())
     ge_out[...] = (dmixed + tn(select[...], back_in[...])).astype(BF16)
+    stores[2].start()
 
     def drain(t):
         m_copy(t, me).wait_send()
@@ -346,6 +379,26 @@
     for peer in peers:
         for copy in dp_copies(peer, dp):
             copy.wait_send()
+    for copy in stores:
+        copy.wait()
+
+
+def export(a, b, c, a_out, b_out, c_out, a_held, b_held, c_held, sems):
+    loads = [
+        pltpu.make_async_copy(source, held, sems.at[i])
+        for i, (source, held) in enumerate(((b, b_held), (c, c_held), (a, a_held)))
+    ]
+    stores = [
+        pltpu.make_async_copy(held, target, sems.at[3 + i])
+        for i, (held, target) in enumerate(((b_held, b_out), (c_held, c_out), (a_held, a_out)))
+    ]
+    for copy in loads:
+        copy.start()
+    for load, store in zip(loads, stores):
+        load.wait()
+        store.start()
+    for copy in stores:
+        copy.wait()
 
 
 def body(n, copies, events, gate_weights, routes, session_of, partner, expert_in, expert_out):
@@ -357,6 +410,7 @@
     slots = n * cap
     dma = pltpu.SemaphoreType.DMA
     vmem = pl.BlockSpec(memory_space=pltpu.VMEM)
+    hbm = pl.BlockSpec(memory_space=pltpu.HBM)
     loss, ge, gi, go = pl.pallas_call(
         functools.partial(kernel, n, copies, cap, sessions),
         out_shape=(
@@ -365,8 +419,8 @@
             jax.ShapeDtypeStruct((part, ff), BF16),
             jax.ShapeDtypeStruct((ff, part), BF16),
         ),
-        in_specs=[vmem] * 7,
-        out_specs=(vmem,) * 4,
+        in_specs=[hbm] * 7,
+        out_specs=(vmem,) + (hbm,) * 3,
         scratch_shapes=[
             pltpu.VMEM((slots, ev), BF16),
             pltpu.VMEM((SUB, ev), F32),
@@ -377,10 +431,10 @@
             pltpu.VMEM((2, n // 2 * SUB, slots // 2), F32),
             pltpu.VMEM((slots, ff), F32),
             pltpu.VMEM((slots, ff), BF16),
-            pltpu.VMEM((n, sessions, width), F32),
-            pltpu.VMEM((n, sessions, width), F32),
-            pltpu.VMEM((sessions, width), F32),
-            pltpu.VMEM((n, sessions, width), F32),
+            pltpu.VMEM((n, sessions, width), BF16),
+            pltpu.VMEM((n, sessions, width), BF16),
+            pltpu.VMEM((sessions, width), BF16),
+            pltpu.VMEM((n, sessions, width), BF16),
             pltpu.VMEM((n * SUB, width), F32),
             pltpu.VMEM((n * SUB, width), F32),
             pltpu.VMEM((slots, width), BF16),
@@ -392,15 +446,43 @@
             pltpu.VMEM((copies, ff, part), BF16),
             pltpu.VMEM((copies, ff, part), BF16),
             pltpu.VMEM((copies, SUB, 128), F32),
+            pltpu.VMEM((slots, width), F32),
+            pltpu.VMEM((ev, width), BF16),
+            pltpu.VMEM((2, ev), F32),
+            pltpu.VMEM((2, ev), jnp.int32),
+            pltpu.VMEM((1, ev), jnp.int32),
+            pltpu.VMEM((1, sessions), jnp.int32),
+            pltpu.VMEM((width, ff), BF16),
+            pltpu.VMEM((ff, width), BF16),
+            pltpu.VMEM((ev, width), BF16),
+            pltpu.VMEM((part, ff), BF16),
+            pltpu.VMEM((ff, part), BF16),
+            dma((7,)),
+            dma((3,)),
         ]
         + [dma((n,))] * 10
         + [dma((copies,))] * 6,
-        compiler_params=pltpu.CompilerParams(collective_id=0, has_side_effects=True, vmem_limit_bytes=50 << 20),
+        compiler_params=pltpu.CompilerParams(collective_id=0, has_side_effects=True, vmem_limit_bytes=VMEM_ALL),
         name="session_moe",
     )(
         events, gate_weights.T, routes.T, session_of.reshape(1, ev), partner.reshape(1, sessions),
         expert_in[0], expert_out[0],
     )
+    ge, gi, go = pl.pallas_call(
+        export,
+        out_shape=(
+            jax.ShapeDtypeStruct((ev, width), BF16),
+            jax.ShapeDtypeStruct((part, ff), BF16),
+            jax.ShapeDtypeStruct((ff, part), BF16),
+        ),
+        in_specs=[hbm] * 3,
+        out_specs=(hbm,) * 3,
+        scratch_shapes=[
+            pltpu.VMEM((ev, width), BF16), pltpu.VMEM((part, ff), BF16), pltpu.VMEM((ff, part), BF16), dma((6,)),
+        ],
+        compiler_params=pltpu.CompilerParams(vmem_limit_bytes=VMEM_ALL),
+        name="export",
+    )(ge, gi, go)
     return loss.reshape(()), ge, gi[None], go[None]
 
 

time: 57.3 us -> 52.5 us (0.916)
  local copies, waits for them, and re-layouts: 6.28 us -> 0 us
  Pallas kernels: 48.4 us -> 49.9 us
    unnamed x17 -> x0, local copies, waits for them, and re-layouts: 6.28 us -> none
    pallas_call x0 -> x1, Pallas kernels: none -> 2.09 us  [body(): pl.pallas_call(export, out_shape=(jax.ShapeDtypeStruct((ev, width), BF16)...]
where the time goes in v2:
time: 52.5 us; the launch traced here: 52.3 us
  Pallas kernels  49.9 us (95%)
  between operations  2.38 us (5%)
    pallas_call x1, Pallas kernels, body(): pl.pallas_call(functools.partial(kernel, n, copies, cap, sessions), out_s...  47.9 us
    pallas_call x1, Pallas kernels, body(): pl.pallas_call(export, out_shape=(jax.ShapeDtypeStruct((ev, width), BF16)...  2.09 us

profile of v2, /device:TPU:0, one launch (start us, length us, event | category | flops | bytes accessed | tf_op | source)
XLA Modules:
  0.0 52.3 jit_solution(12984228266422698653)
XLA Ops:
  0.6 47.9 %session_moe.1 = (f32[1,1]{1,0:T(1,128)}, bf16[128,512]{1,0:T(8,128)(2,1)}, bf16[256,1024]{1,0:T(8,128)(2,1)}, bf16[1024,256]{1,0:T(8,128)(2,1)}) custom-call(bf16[128,512]{1,0:T(8,128)(2,1)} %events_h.1, f32[2,128]{1,0:T(2,128)} %bitcast.11, s32[2,128]{1,0:T(2,128)} %bitcast.12, s32[1,128]{1,0:T(1,128)} %bitcast.13, s32[1,4]{1,0:T(1,128)} %bitcast.14, ...), custom_call_target="tpu_custom_call" | custom-call | tf_op jit(solution)/shard_map/session_moe/pallas_call | solution.py:414
  48.5 2.1 %export.1 = (bf16[128,512]{1,0:T(8,128)(2,1)}, bf16[256,1024]{1,0:T(8,128)(2,1)}, bf16[1024,256]{1,0:T(8,128)(2,1)}) custom-call(bf16[128,512]{1,0:T(8,128)(2,1)} %get-tuple-element.12.a, bf16[256,1024]{1,0:T(8,128)(2,1)} %get-tuple-element.13.b, bf16[1024,256]{1,0:T(8,128)(2,1)} %get-tuple-element.14.c), custom_call_target="tpu_custom_call" | custom-call | tf_op jit(solution)/shard_map/export/pallas_call | solution.py:471

commit v3 on v2

--- a/solution.py
+++ b/solution.py
@@ -45,7 +45,7 @@
     n, copies, cap, sessions,
     events_h, gates_h, routes_h, session_h, partner_h, w_in_h, w_out_h,
     loss_out, ge_h, gi_h, go_h,
-    select, member_s, outbox, inbox, meta_out, meta_in, block, pre, hidden,
+    select, member_s, outbox, inbox, meta_out, meta_in, meta_all, block, pre, hidden,
     pool_out, pool_in, emb_out, emb_in, emb_all, dm_all, dy_s, dpre_s, back_out, back_in,
     gi_out, gi_in, go_out, go_in, loss_buf, gate_cols,
     events, gates, routes, session_of, partner, w_in, w_out, ge_out, gi_final, go_final, fetch, store,
@@ -109,13 +109,76 @@
     outbox[...] = nn(select[...], events[...]).astype(BF16)
     member = jnp.where(iota((SUB, ev), 0) == session_of[...], 1.0, 0.0).astype(F32)
     member_s[...] = member
+    member_b = member.astype(BF16)
     counts = jnp.sum(member, axis=1, keepdims=True)
     own_partner = jnp.sum(
         jnp.where(iota((SUB, sessions), 0) == iota((SUB, sessions), 1), partner[...], 0).astype(F32),
         axis=1, keepdims=True,
     )
+    pl.semaphore_wait(barrier, n - 1 + copies - 1)
+
+    def span(e):
+        return pl.ds(pl.multiple_of(e * cap, cap), cap)
+
+    def x_copy(target, source):
+        return pltpu.make_async_remote_copy(
+            src_ref=outbox.at[span(target)], dst_ref=inbox.at[span(source)],
+            send_sem=x_send.at[target], recv_sem=x_recv.at[source],
+            device_id={"expert": target}, device_id_type=MESH,
+        )
+
+    def m_copy(target, source):
+        return pltpu.make_async_remote_copy(
+            src_ref=meta_out.at[target], dst_ref=meta_in.at[source],
+            send_sem=m_send.at[target], recv_sem=m_recv.at[source],
+            device_id={"expert": target}, device_id_type=MESH,
+        )
+
+    def p_copy(target, source):
+        return pltpu.make_async_remote_copy(
+            src_ref=pool_out.at[target], dst_ref=pool_in.at[source],
+            send_sem=p_send.at[target], recv_sem=p_recv.at[source],
+            device_id={"expert": target}, device_id_type=MESH,
+        )
+
+    def e_copy(target, source):
+        return pltpu.make_async_remote_copy(
+            src_ref=emb_out, dst_ref=emb_in.at[source],
+            send_sem=e_send.at[target], recv_sem=e_recv.at[source],
+            device_id={"expert": target}, device_id_type=MESH,
+        )
+
+    def d_copy(target, source):
+        return pltpu.make_async_remote_copy(
+            src_ref=back_out.at[span(target)], dst_ref=back_in.at[span(source)],
+            send_sem=d_send.at[target], recv_sem=d_recv.at[source],
+            device_id={"expert": target}, device_id_type=MESH,
+        )
+
+    def in_far(i):
+        return far * half_n + lax.rem(me + i, half_n)
+
+    def in_near(i):
+        return my_half * half_n + lax.rem(me + i, half_n)
+
+    def each_far(act):
+        def step(i, _):
+            act(in_far(i))
+            return 0
+
+        lax.fori_loop(0, half_n, step, 0)
+
+    def each_near(act):
+        def step(i, _):
+            act(in_near(i))
+            return 0
+
+        lax.fori_loop(1, half_n, step, 0)
+
+    each_far(lambda t: x_copy(t, me).start())
+    each_near(lambda t: x_copy(t, me).start())
+
     gate_high, gate_low = halves(gate_at)
-    member_b = member.astype(BF16)
     lane = iota((SUB, 128), 1)
     wide = nt(member_b, gate_high) + nt(member_b, gate_low)
     for e in range(n):
@@ -125,76 +188,12 @@
             tile = pltpu.roll(tile, 128 - offset, 1)
         tile = jnp.where(lane < cap, tile, 0.0)
         tile = jnp.where(lane == COUNT_LANE, counts, tile)
-        meta_out[e] = jnp.where(lane == PARTNER_LANE, own_partner, tile)
-
-    pl.semaphore_wait(barrier, n - 1 + copies - 1)
-
-    def span(e):
-        return pl.ds(pl.multiple_of(e * cap, cap), cap)
-
-    def x_copy(target, source):
-        return pltpu.make_async_remote_copy(
-            src_ref=outbox.at[span(target)], dst_ref=inbox.at[span(source)],
-            send_sem=x_send.at[target], recv_sem=x_recv.at[source],
-            device_id={"expert": target}, device_id_type=MESH,
-        )
-
-    def m_copy(target, source):
-        return pltpu.make_async_remote_copy(
-            src_ref=meta_out.at[target], dst_ref=meta_in.at[source],
-            send_sem=m_send.at[target], recv_sem=m_recv.at[source],
-            device_id={"expert": target}, device_id_type=MESH,
-        )
-
-    def p_copy(target, source):
-        return pltpu.make_async_remote_copy(
-            src_ref=pool_out.at[target], dst_ref=pool_in.at[source],
-            send_sem=p_send.at[target], recv_sem=p_recv.at[source],
-            device_id={"expert": target}, device_id_type=MESH,
-        )
-
-    def e_copy(target, source):
-        return pltpu.make_async_remote_copy(
-            src_ref=emb_out, dst_ref=emb_in.at[source],
-            send_sem=e_send.at[target], recv_sem=e_recv.at[source],
-            device_id={"expert": target}, device_id_type=MESH,
-        )
-
-    def d_copy(target, source):
-        return pltpu.make_async_remote_copy(
-            src_ref=back_out.at[span(target)], dst_ref=back_in.at[span(source)],
-            send_sem=d_send.at[target], recv_sem=d_recv.at[source],
-            device_id={"expert": target}, device_id_type=MESH,
-        )
-
-    def in_far(i):
-        return far * half_n + lax.rem(me + i, half_n)
-
-    def in_near(i):
-        return my_half * half_n + lax.rem(me + i, half_n)
-
-    def each_far(act):
-        def step(i, _):
-            act(in_far(i))
-            return 0
-
-        lax.fori_loop(0, half_n, step, 0)
-
-    def each_near(act):
-        def step(i, _):
-            act(in_near(i))
-            return 0
-
-        lax.fori_loop(1, half_n, step, 0)
-
-    def send_x(t):
-        m_copy(t, me).start()
-        x_copy(t, me).start()
-
-    each_far(send_x)
-    each_near(send_x)
+        meta_out[e] = jnp.where(lane == PARTNER_LANE, own_partner, tile)[0:sessions]
+    each_far(lambda t: m_copy(t, me).start())
+    each_near(lambda t: m_copy(t, me).start())
     inbox[span(me), :] = outbox[span(me), :]
     meta_in[me] = meta_out[me]
+    no_rows = jnp.zeros((SUB - sessions, 128), F32)
 
     event_sum = nn(member_b, events[...])
 
@@ -209,7 +208,10 @@
         act = (preact / (1.0 + jnp.exp(-preact))).astype(BF16)
         hidden[at, :] = act
         y = nn(act, w_out[...]).astype(BF16)
-        table = meta_in[pl.ds(half * half_n, half_n)].reshape(ses_rows, 128)
+        for j in range(half_n):
+            e = half * half_n + j
+            meta_all[e] = jnp.concatenate([meta_in[e], no_rows], axis=0)
+        table = meta_all[pl.ds(half * half_n, half_n)].reshape(ses_rows, 128)
         spread = jnp.where(iota((128, rows), 0) == iota((128, rows), 1) % cap, 1.0, 0.0).astype(BF16)
         high, low = halves(table)
         full = nn(high, spread) + nn(low, spread)
@@ -262,7 +264,7 @@
     rscale = lax.rsqrt(jnp.mean(emb * emb, axis=1, keepdims=True) + EPS)
     unit = emb * rscale
     zemb = unit.astype(BF16)
-    table = meta_in[...].reshape(batch, 128)
+    table = meta_all[...].reshape(batch, 128)
     table_lane = iota((batch, 128), 1)
     row1 = iota((batch, 1), 0)
     real1 = row1 % SUB < sessions
@@ -289,19 +291,31 @@
     dpooled = rscale * (dunit - unit * jnp.mean(dunit * unit, axis=1, keepdims=True))
     dm_all[...] = dpooled / number
 
-    def backward(half):
-        at = pl.ds(pl.multiple_of(half * rows, rows), rows)
-        high, low = halves(dm_all[pl.ds(pl.multiple_of(half * ses_rows, ses_rows), ses_rows), :])
-        hot = jnp.where(block[half] != 0.0, 1.0, 0.0).astype(BF16)
+    q_rows, q_ses, q_n = rows // 2, ses_rows // 2, half_n // 2
+
+    def backward(half, q):
+        at = pl.ds(pl.multiple_of(half * rows + q * q_rows, q_rows), q_rows)
+        high, low = halves(dm_all[pl.ds(pl.multiple_of(half * ses_rows + q * q_ses, q_ses), q_ses), :])
+        full = block[half, q * q_ses : (q + 1) * q_ses, q * q_rows : (q + 1) * q_rows]
+        hot = jnp.where(full != 0.0, 1.0, 0.0).astype(BF16)
         dy = ((tn(hot, high) + tn(hot, low)) * gate_cols[at, :]).astype(BF16)
         dy_s[at, :] = dy
         dpre = (nt(dy, w_out[...]) * pre[at, :]).astype(BF16)
         dpre_s[at, :] = dpre
         back_out[at, :] = nt(dpre, w_in[...]).astype(BF16)
 
-    backward(far)
-    each_far(lambda t: d_copy(t, me).start())
-    backward(my_half)
+    def send_quarter(q):
+        def step(i, _):
+            d_copy(far * half_n + q * q_n + lax.rem(me + i, q_n), me).start()
+            return 0
+
+        lax.fori_loop(0, q_n, step, 0)
+
+    for q in range(2):
+        backward(far, q)
+        send_quarter(q)
+    for q in range(2):
+        backward(my_half, q)
     each_near(lambda t: d_copy(t, me).start())
     back_in[span(me), :] = back_out[span(me), :]
 
@@ -426,7 +440,8 @@
             pltpu.VMEM((SUB, ev), F32),
             pltpu.VMEM((slots, width), BF16),
             pltpu.VMEM((slots, width), BF16),
-            pltpu.VMEM((n, SUB, 128), F32),
+            pltpu.VMEM((n, sessions, 128), F32),
+            pltpu.VMEM((n, sessions, 128), F32),
             pltpu.VMEM((n, SUB, 128), F32),
             pltpu.VMEM((2, n // 2 * SUB, slots // 2), F32),
             pltpu.VMEM((slots, ff), F32),

time: 52.5 us -> 49.5 us (0.943)
  Pallas kernels: 49.9 us -> 47 us
    pallas_call x1, Pallas kernels: 47.9 us -> 44.9 us  [body(): pl.pallas_call(functools.partial(kernel, n, copies, cap, sessions), out_s...]
where the time goes in v3:
time: 49.5 us; the launch traced here: 49.3 us
  Pallas kernels  47 us (95%)
  between operations  2.38 us (5%)
    pallas_call x1, Pallas kernels, body(): pl.pallas_call(functools.partial(kernel, n, copies, cap, sessions), out_s...  44.9 us
    pallas_call x1, Pallas kernels, body(): pl.pallas_call(export, out_shape=(jax.ShapeDtypeStruct((ev, width), BF16)...  2.09 us

profile of v3, /device:TPU:0, one launch (start us, length us, event | category | flops | bytes accessed | tf_op | source)
XLA Modules:
  0.0 49.3 jit_solution(17193125680074762220)
XLA Ops:
  0.6 44.9 %session_moe.1 = (f32[1,1]{1,0:T(1,128)}, bf16[128,512]{1,0:T(8,128)(2,1)}, bf16[256,1024]{1,0:T(8,128)(2,1)}, bf16[1024,256]{1,0:T(8,128)(2,1)}) custom-call(bf16[128,512]{1,0:T(8,128)(2,1)} %events_h.1, f32[2,128]{1,0:T(2,128)} %bitcast.11, s32[2,128]{1,0:T(2,128)} %bitcast.12, s32[1,128]{1,0:T(1,128)} %bitcast.13, s32[1,4]{1,0:T(1,128)} %bitcast.14, ...), custom_call_target="tpu_custom_call" | custom-call | tf_op jit(solution)/shard_map/session_moe/pallas_call | solution.py:428
  45.5 2.1 %export.1 = (bf16[128,512]{1,0:T(8,128)(2,1)}, bf16[256,1024]{1,0:T(8,128)(2,1)}, bf16[1024,256]{1,0:T(8,128)(2,1)}) custom-call(bf16[128,512]{1,0:T(8,128)(2,1)} %get-tuple-element.12.a, bf16[256,1024]{1,0:T(8,128)(2,1)} %get-tuple-element.13.b, bf16[1024,256]{1,0:T(8,128)(2,1)} %get-tuple-element.14.c), custom_call_target="tpu_custom_call" | custom-call | tf_op jit(solution)/shard_map/export/pallas_call | solution.py:486
